TPU v7x, 32 devices: a whole 2x2x4 slice. The times are simulated.
32 devices in a mesh: tensor: 4 (over y, x), expert: 8 (over z, core).
Axes of the slice: x: 2, y: 2, z: 4, core: 2. Of those that a mesh axis runs over, the one named last changes fastest.
Arguments:
- tokens: bfloat16 [16, 1024, 768], P('expert', 'tensor'), may hold values from -6 to 6
- out_grad: bfloat16 [16, 1024, 768], P('expert', 'tensor'), may hold values from -6 to 6
- masked: int32 [16, 1024], P('expert', 'tensor'), may hold values from 0 to 1, as said below
- route: int32 [16, 1024, 1], P('expert', 'tensor'), may hold values from 0 to 3
- norm1_gain: float32 [768], replicated, may hold values from 0.5 to 1.5
- query_key_value_weight: bfloat16 [3, 768, 768], P(None, None, 'tensor'), may hold values from -0.625 to 0.625
- output_weight: bfloat16 [768, 768], P('tensor'), may hold values from -5 to 5
- norm2_gain: float32 [768], replicated, may hold values from 0.5 to 1.5
- route_weight: float32 [768, 16], replicated, may hold values from -0.21875 to 0.21875
- expert_embed: float32 [4, 16], replicated, may hold values from -6 to 6
- up_weight: bfloat16 [8, 768, 1536], P('expert'), may hold values from -0.21875 to 0.21875
- down_weight: bfloat16 [8, 768, 1536], P('expert'), may hold values from -1 to 1
Outputs:
- out: float32 [16, 1024, 768], P('expert', 'tensor')
- input_grad: float32 [16, 1024, 768], P('expert', 'tensor')
- loads: float32 [4], replicated
- norm1_grad: float32 [768], replicated
- query_key_value_gradient: float32 [3, 768, 768], P(None, None, 'tensor')
- out_proj_grad: float32 [768, 768], P('tensor')
- norm2_grad: float32 [768], replicated
- route_weight_grad: float32 [768, 16], replicated
- embed_grad: float32 [4, 16], replicated
- up_weight_grad: float32 [8, 768, 1536], P('expert', None, 'tensor')
- down_weight_grad: float32 [8, 768, 1536], P('expert', None, 'tensor')
Inputs may be any that keep to these rules, and one draw needn't show every extreme that they name: 1 marks a masked position; only these carry a gradient. Every expert is the route of some token.
All inputs are finite; a program needn't handle non-finite values.
Results may differ from a plain program's by a relative error of at most 0.015.
The roundings to bfloat16 on the way count: a program that leaves them out, or rounds other values in their place, can miss the bound.
Values may be sent and summed in bfloat16 or wider, within the bound.
No kernel may reach another device: no remote copies, remote signals or barrier semaphores. Data moves between devices by JAX's collectives and lax.ppermute only.
A program may use at most 192 MiB of HBM per device.

v0:
```python
from functools import partial
import jax
import jax.numpy as jnp
from jax import lax
from jax.sharding import PartitionSpec as P

HEAD = 64


def layer_norm(values, gain):
    center = values - jnp.mean(values, axis=-1, keepdims=True)
    spread = jnp.mean(center * center, axis=-1, keepdims=True)
    return center * lax.rsqrt(spread + 1e-05) * gain


def unit_rows(values):
    return values * lax.rsqrt(jnp.sum(values * values, axis=-1, keepdims=True) + 1e-06)


def gelu_exact(values):
    return jax.nn.gelu(values, approximate=False)


def pair_copy(values):
    count = values.shape[0]
    return jnp.broadcast_to(values[:, None], (count, 2) + values.shape[1:]).reshape(
        (2 * count,) + values.shape[1:]
    )


def pair_total(values):
    count = values.shape[0] // 2
    return jnp.sum(values.reshape((count, 2) + values.shape[1:]), axis=1)


def route_gate(normed, route_weight, expert_embed, picked):
    rows = unit_rows(jnp.dot(normed, route_weight, precision=lax.Precision.HIGHEST))
    centers = unit_rows(expert_embed)
    logits = 3.0 * jnp.dot(rows, centers.T, precision=lax.Precision.HIGHEST)
    probs = jax.nn.softmax(logits, axis=-1)
    return jnp.sum(probs * picked, axis=-1)


def attend_forward(query, key_all, value_all, score_scale):
    scores = (
        jnp.einsum("bhe,khe->hbk", query, key_all, preferred_element_type=jnp.float32) * score_scale
    )
    top = jnp.max(scores, axis=-1, keepdims=True)
    expos = jnp.exp(scores - top)
    total = jnp.sum(expos, axis=-1, keepdims=True)
    probs = (expos / total).astype(jnp.bfloat16)
    mixed = jnp.einsum("hbk,khe->bhe", probs, value_all, preferred_element_type=jnp.float32)
    return (mixed.astype(jnp.bfloat16), (top + jnp.log(total))[..., 0])


def attend_backward(query, key_all, value_all, grad_mixed, log_total, score_scale):
    scores = (
        jnp.einsum("bhe,khe->hbk", query, key_all, preferred_element_type=jnp.float32) * score_scale
    )
    probs = jnp.exp(scores - log_total[..., None])
    probs_low = probs.astype(jnp.bfloat16)
    grad_probs = jnp.einsum(
        "bhe,khe->hbk", grad_mixed, value_all, preferred_element_type=jnp.float32
    )
    inner = jnp.sum(probs * grad_probs, axis=-1, keepdims=True)
    grad_scores = (probs * (grad_probs - inner)).astype(jnp.bfloat16)
    query_part = (
        jnp.einsum("hbk,khe->bhe", grad_scores, key_all, preferred_element_type=jnp.float32)
        * score_scale
    )
    key_part = (
        jnp.einsum("hbk,bhe->khe", grad_scores, query, preferred_element_type=jnp.float32)
        * score_scale
    )
    value_part = jnp.einsum(
        "hbk,bhe->khe", probs_low, grad_mixed, preferred_element_type=jnp.float32
    )
    return (query_part, key_part, value_part)


def body(
    tokens,
    out_grad,
    masked,
    route,
    norm1_gain,
    query_key_value_weight,
    output_weight,
    norm2_gain,
    route_weight,
    expert_embed,
    up_weight,
    down_weight,
):
    seq_count, shard_len, features = tokens.shape
    rows_here = seq_count * shard_len
    experts = expert_embed.shape[0]
    capacity = rows_here // experts
    channels = query_key_value_weight.shape[2]
    head_count = channels // HEAD
    score_scale = HEAD ** (-0.5)
    contract_rows = (((0,), (0,)), ((), ()))
    contract_cols = (((1,), (1,)), ((), ()))
    inputs = tokens.astype(jnp.float32).reshape(rows_here, features)
    normed_one, norm_one_pull = jax.vjp(layer_norm, inputs, norm1_gain)
    normed_low = normed_one.astype(jnp.bfloat16).reshape(seq_count, shard_len, features)
    collected_rows = lax.all_gather(normed_low, "tensor", axis=1, tiled=True)
    seq_len = collected_rows.shape[1]
    block = min(512, seq_len)
    projected = jnp.einsum(
        "wxa,cam->cwxm", collected_rows, query_key_value_weight, preferred_element_type=jnp.float32
    ).astype(jnp.bfloat16)
    heads_view = projected.reshape(3, seq_count, seq_len, head_count, HEAD)
    mixed_seqs = []
    total_rows = []
    for sequence in range(seq_count):
        key_all = heads_view[1, sequence]
        value_all = heads_view[2, sequence]
        mixed_blocks = []
        total_blocks = []
        for start_row in range(0, seq_len, block):
            mixed_blk, total_blk = attend_forward(
                heads_view[0, sequence, start_row : start_row + block],
                key_all,
                value_all,
                score_scale,
            )
            mixed_blocks.append(mixed_blk)
            total_blocks.append(total_blk)
        mixed_seqs.append(jnp.concatenate(mixed_blocks, axis=0))
        total_rows.append(jnp.concatenate(total_blocks, axis=1))
    mixed_everything = jnp.stack(mixed_seqs, axis=0).reshape(seq_count, seq_len, channels)
    piece = mixed_everything
    attn = lax.psum_scatter(
        jnp.einsum("slh,hd->lsd", piece, output_weight, preferred_element_type=jnp.float32),
        "tensor",
        scatter_dimension=0,
        tiled=True,
    )
    hidden = inputs + attn.transpose(1, 0, 2).reshape(rows_here, features)
    normed_two, norm_two_pull = jax.vjp(layer_norm, hidden, norm2_gain)
    picks = route.reshape(rows_here)
    expert_ids = jnp.arange(experts, dtype=jnp.int32)
    member = (picks[:, None] == expert_ids[None, :]).astype(jnp.int32)
    earlier = jnp.cumsum(member, axis=0) - member
    slot_ids = jnp.sum(earlier * member, axis=1)
    target = picks * capacity + slot_ids
    slot_range = jnp.arange(experts * capacity, dtype=jnp.int32)
    placing = ((slot_range[:, None] == target[None, :]) & (slot_ids < capacity)[None, :]).astype(
        jnp.bfloat16
    )
    gate, gate_pull = jax.vjp(
        partial(route_gate, picked=member.astype(jnp.float32)),
        normed_two,
        route_weight,
        expert_embed,
    )
    sent = jnp.dot(
        placing, normed_two.astype(jnp.bfloat16), preferred_element_type=jnp.float32
    ).astype(jnp.bfloat16)
    received = lax.all_to_all(
        pair_copy(sent.reshape(experts, capacity, features)),
        "expert",
        split_axis=0,
        concat_axis=0,
        tiled=True,
    )
    recv_rows = received.shape[0] * capacity
    slot_block = received.reshape(recv_rows, features)
    up = jnp.dot(slot_block, up_weight[0], preferred_element_type=jnp.float32)
    active, act_pull = jax.vjp(gelu_exact, up)
    active_low = active.astype(jnp.bfloat16)
    returned = lax.dot_general(
        active_low, down_weight[0], contract_cols, preferred_element_type=jnp.float32
    )
    back = lax.all_to_all(
        returned.reshape(received.shape).astype(jnp.bfloat16),
        "expert",
        split_axis=0,
        concat_axis=0,
        tiled=True,
    ).astype(jnp.float32)
    back_low = pair_total(back).astype(jnp.bfloat16)
    mixture = lax.dot_general(
        placing,
        back_low.reshape(experts * capacity, features),
        contract_rows,
        preferred_element_type=jnp.float32,
    )
    result = hidden + gate[:, None] * mixture
    grad_out = out_grad.astype(jnp.float32).reshape(rows_here, features) * masked.reshape(
        rows_here, 1
    ).astype(jnp.float32)
    grad_gate = jnp.sum(grad_out * mixture, axis=1)
    grad_mixture = (gate[:, None] * grad_out).astype(jnp.bfloat16)
    grad_sent = jnp.dot(placing, grad_mixture, preferred_element_type=jnp.float32).astype(
        jnp.bfloat16
    )
    grad_received = lax.all_to_all(
        pair_copy(grad_sent.reshape(experts, capacity, features)),
        "expert",
        split_axis=0,
        concat_axis=0,
        tiled=True,
    )
    grad_rows_in = grad_received.reshape(recv_rows, features)
    grad_active = jnp.dot(grad_rows_in, down_weight[0], preferred_element_type=jnp.float32)
    grad_up = act_pull(grad_active)[0].astype(jnp.bfloat16)
    down_full = lax.dot_general(
        grad_rows_in, active_low, contract_rows, preferred_element_type=jnp.float32
    )
    up_full = lax.dot_general(
        slot_block, grad_up, contract_rows, preferred_element_type=jnp.float32
    )
    grad_slots = lax.dot_general(
        grad_up, up_weight[0], contract_cols, preferred_element_type=jnp.float32
    )
    up_weight_grad, down_weight_grad = (
        lax.psum_scatter(
            up_full.astype(jnp.bfloat16), "tensor", scatter_dimension=1, tiled=True
        ).astype(jnp.float32),
        lax.psum_scatter(
            down_full.astype(jnp.bfloat16), "tensor", scatter_dimension=1, tiled=True
        ).astype(jnp.float32),
    )
    grad_back = lax.all_to_all(
        grad_slots.reshape(received.shape).astype(jnp.bfloat16),
        "expert",
        split_axis=0,
        concat_axis=0,
        tiled=True,
    ).astype(jnp.float32)
    grad_back_low = pair_total(grad_back).astype(jnp.bfloat16)
    grad_normed = lax.dot_general(
        placing,
        grad_back_low.reshape(experts * capacity, features),
        contract_rows,
        preferred_element_type=jnp.float32,
    )
    grad_from_gate, route_weight_grad, embed_grad = gate_pull(grad_gate)
    grad_hidden_norm, norm2_grad = norm_two_pull(grad_normed + grad_from_gate)
    grad_hidden = grad_out + grad_hidden_norm
    grad_shard = grad_hidden.astype(jnp.bfloat16).reshape(seq_count, shard_len, features)
    gradient_complete = lax.all_gather(grad_shard, "tensor", axis=1, tiled=True)
    out_proj_local = jnp.einsum(
        "wif,wij->fj", mixed_everything, gradient_complete, preferred_element_type=jnp.float32
    )
    grad_mixed = jnp.einsum(
        "abc,qc->abq", gradient_complete, output_weight, preferred_element_type=jnp.float32
    ).astype(jnp.bfloat16)
    grad_mixed = grad_mixed.reshape(seq_count, seq_len, head_count, HEAD)
    grad_seqs = []
    for sequence in range(seq_count):
        key_all = heads_view[1, sequence]
        value_all = heads_view[2, sequence]
        grad_key = jnp.zeros((seq_len, head_count, HEAD), jnp.float32)
        grad_value = jnp.zeros((seq_len, head_count, HEAD), jnp.float32)
        query_grads = []
        for start_row in range(0, seq_len, block):
            query_part, key_part, value_part = attend_backward(
                heads_view[0, sequence, start_row : start_row + block],
                key_all,
                value_all,
                grad_mixed[sequence, start_row : start_row + block],
                total_rows[sequence][:, start_row : start_row + block],
                score_scale,
            )
            query_grads.append(query_part)
            grad_key = grad_key + key_part
            grad_value = grad_value + value_part
        grad_seqs.append(
            jnp.stack([jnp.concatenate(query_grads, axis=0), grad_key, grad_value], axis=0)
        )
    gradient_projected = (
        jnp.stack(grad_seqs, axis=1).astype(jnp.bfloat16).reshape(3, seq_count, seq_len, channels)
    )
    projection_local = jnp.einsum(
        "pwe,apwu->aeu", collected_rows, gradient_projected, preferred_element_type=jnp.float32
    )
    query_key_value_gradient, out_proj_grad = lax.psum((projection_local, out_proj_local), "expert")
    piece = gradient_projected
    grad_normed_one = lax.psum_scatter(
        jnp.einsum(
            "kslh,kdh->lsd", piece, query_key_value_weight, preferred_element_type=jnp.float32
        ).astype(jnp.bfloat16),
        "tensor",
        scatter_dimension=0,
        tiled=True,
    ).astype(jnp.float32)
    grad_inputs_norm, norm1_grad = norm_one_pull(
        grad_normed_one.transpose(1, 0, 2).reshape(rows_here, features)
    )
    input_grad = grad_hidden + grad_inputs_norm
    loads_local = jnp.sum(member, axis=0).astype(jnp.float32)
    norm1_grad, norm2_grad, route_weight_grad, embed_grad, loads = lax.psum(
        (norm1_grad, norm2_grad, route_weight_grad, embed_grad, loads_local), ("tensor", "expert")
    )
    return (
        result.reshape(seq_count, shard_len, features),
        input_grad.reshape(seq_count, shard_len, features),
        loads,
        norm1_grad,
        query_key_value_gradient,
        out_proj_grad,
        norm2_grad,
        route_weight_grad,
        embed_grad,
        up_weight_grad[None],
        down_weight_grad[None],
    )


def solution(mesh):
    return jax.shard_map(
        body,
        mesh=mesh,
        in_specs=(
            P("expert", "tensor", None),
            P("expert", "tensor", None),
            P("expert", "tensor"),
            P("expert", "tensor", None),
            P(),
            P(None, None, "tensor"),
            P("tensor", None),
            P(),
            P(),
            P(),
            P("expert", None, None),
            P("expert", None, None),
        ),
        out_specs=(
            P("expert", "tensor", None),
            P("expert", "tensor", None),
            P(),
            P(),
            P(None, None, "tensor"),
            P("tensor", None),
            P(),
            P(),
            P(),
            P("expert", None, "tensor"),
            P("expert", None, "tensor"),
        ),
        check_vma=False,
    )
```

profile of v0, /device:TPU:0, one launch (start us, length us, event | category | flops | bytes accessed | tf_op | source)
XLA Modules:
  0.0 632.9 jit_solution(8095519388316317315)
XLA Ops:
  12.0 2.3 fusion.75
  14.4 46.8 %all-gather.3.cloned.1.call-done = bf16[2,1024,768]{2,1,0:T(8,128)(2,1)} async-done(((bf16[2,256,768]{2,1,0:T(8,128)(2,1)}), bf16[2,1024,768]{2,1,0:T(8,128)(2,1)}) %all-gather.3.cloned.1.call-update) | async-done | bytes 3145744 | tf_op jit(solution)/shard_map/all_gather | solution.py:107
  61.2 3.9 fusion.49
  76.9 1.8 fusion.107
  82.7 3.7 convolution_bitcast_fusion
  89.4 67.4 %reduce-scatter.9.cloned.1.call-done = f32[256,2,768]{2,0,1:T(8,128)} async-done(((f32[1024,2,768]{2,0,1:T(8,128)}), f32[256,2,768]{2,0,1:T(8,128)}) %reduce-scatter.9.cloned.1.call-update) | async-done | bytes 1572880 | tf_op jit(solution)/shard_map/reduce_scatter | solution.py:134
  156.8 1.8 fusion.113
  161.4 42.2 %all_to_all.20 = bf16[8,128,768]{2,1,0:T(8,128)(2,1)S(1)} all-to-all(bf16[8,128,768]{2,1,0:T(8,128)(2,1)S(1)} %bitcast.361), channel_id=1, replica_groups=mesh['tensor'=4,'expert'=8] {'expert'}, dimensions={0} | all-to-all | bytes 3145728 | tf_op jit(solution)/shard_map/all_to_all | solution.py:161
  203.7 18.1 %multiply_convert_fusion.4 = (bf16[1024,1536]{1,0:T(8,128)(2,1)S(1)}, f32[1024,1536]{1,0:T(8,128)}, f32[1024,1536]{1,0:T(8,128)}) fusion(bf16[1024,768]{1,0:T(8,128)(2,1)S(1)} %bitcast.378, bf16[1,768,1536]{2,1,0:T(8,128)(2,1)S(1)} %copy-done), kind=kOutput, calls=%fused_computation.16 | convolution fusion | flops 2518155264 | bytes 19660800 | tf_op jit(solution)/shard_map/dot_general | solution.py:170
  221.8 1.7 copy-done.126
  223.5 3.7 fusion.52
  227.2 4.9 all-to-all-start.1
  232.8 3.1 multiply_reduce_fusion.12
  237.4 32.5 %all-to-all-done.1 = bf16[8,128,768]{2,1,0:T(8,128)(2,1)} async-done(((bf16[8,128,768]{2,1,0:T(8,128)(2,1)}), bf16[8,128,768]{2,1,0:T(8,128)(2,1)}, u32[]{:S(2)}, u32[]{:S(2)}) %all-to-all-start.1) | async-done | bytes 1572896 | tf_op jit(solution)/shard_map/all_to_all | solution.py:176
  269.9 1.6 bitcast_reduce_fusion.1
  271.6 2.4 fusion.66
  275.7 40.4 %all_to_all.21 = bf16[8,128,768]{2,1,0:T(8,128)(2,1)S(1)} all-to-all(bf16[8,128,768]{2,1,0:T(8,128)(2,1)S(1)} %bitcast.362), channel_id=1, replica_groups=mesh['tensor'=4,'expert'=8] {'expert'}, dimensions={0} | all-to-all | bytes 3145728 | tf_op jit(solution)/shard_map/all_to_all | solution.py:199
  316.1 7.5 %add_convert_fusion = bf16[1024,1536]{1,0:T(8,128)(2,1)S(1)} fusion(f32[1024,1536]{1,0:T(8,128)} %get-tuple-element.29, f32[1024,1536]{1,0:T(8,128)} %get-tuple-element.47, bf16[1024,768]{1,0:T(8,128)(2,1)S(1)} %bitcast.380, bf16[1,768,1536]{2,1,0:T(8,128)(2,1)S(1)} %copy-done.123), kind=kOutput, calls=%fused_computation.15 | convolution fusion | flops 2437939200 | bytes 19660800 | tf_op jit(solution)/shard_map/dot_general | solution.py:207
  323.6 1.7 copy-done.127
  325.3 3.7 fusion.55
  329.1 4.5 all-to-all-start.3
  334.6 36.7 %all-to-all-done.3 = bf16[8,128,768]{2,1,0:T(8,128)(2,1)} async-done(((bf16[8,128,768]{2,1,0:T(8,128)(2,1)}), bf16[8,128,768]{2,1,0:T(8,128)(2,1)}, u32[]{:S(2)}, u32[]{:S(2)}) %all-to-all-start.3) | async-done | bytes 1572896 | tf_op jit(solution)/shard_map/all_to_all | solution.py:226
  371.3 1.6 bitcast_reduce_fusion
  374.5 3.2 multiply_reduce_fusion.8
  377.7 1.8 fusion.200
  382.1 6.4 %convolution_convert_fusion = bf16[768,1536]{1,0:T(8,128)(2,1)} fusion(bf16[1024,768]{1,0:T(8,128)(2,1)} %bitcast.381, bf16[1024,1536]{1,0:T(8,128)(2,1)} %copy-done.126), kind=kOutput, calls=%fused_computation.50 | convolution fusion | flops 2417098752 | bytes 7077888 | tf_op jit(solution)/shard_map/dot_general | solution.py:209
  388.6 4.4 copy.71
  393.2 6.4 %convolution_convert_fusion.1 = bf16[768,1536]{1,0:T(8,128)(2,1)} fusion(bf16[1024,768]{1,0:T(8,128)(2,1)} %bitcast.379, bf16[1024,1536]{1,0:T(8,128)(2,1)} %copy-done.127), kind=kOutput, calls=%fused_computation.51 | convolution fusion | flops 2417098752 | bytes 7077888 | tf_op jit(solution)/shard_map/dot_general | solution.py:212
  399.6 4.3 copy.69
  404.0 19.9 %all-gather.5.cloned.1.call-done = bf16[2,1024,768]{2,1,0:T(8,128)(2,1)} async-done(((bf16[2,256,768]{2,1,0:T(8,128)(2,1)}), bf16[2,1024,768]{2,1,0:T(8,128)(2,1)}) %all-gather.5.cloned.1.call-update) | async-done | bytes 3145744 | tf_op jit(solution)/shard_map/all_gather | solution.py:244
  423.9 3.2 convolution_convert_fusion.2
  427.1 4.3 multiply_reduce_fusion
  431.4 4.2 multiply_convert_fusion
  436.7 2.1 multiply_reduce_fusion.1
  441.6 3.8 multiply_reduce_fusion.2
  445.4 3.9 multiply_convert_fusion.2
  450.3 3.8 multiply_reduce_fusion.3
  454.9 3.8 multiply_convert_fusion.3
  470.5 4.1 fusion.22
  476.9 1.8 fusion.121
  480.2 24.4 %reduce-scatter.13.cloned.1.call-done = bf16[384,768]{1,0:T(8,128)(2,1)} async-done(((bf16[1536,768]{1,0:T(8,128)(2,1)}), bf16[384,768]{1,0:T(8,128)(2,1)}) %reduce-scatter.13.cloned.1.call-update) | async-done | bytes 589840
  510.4 3.4 fusion.78
  513.9 37.5 %reduce-scatter.11.cloned.1.call-done = bf16[256,2,768]{2,0,1:T(8,128)(2,1)} async-done(((bf16[1024,2,768]{2,0,1:T(8,128)(2,1)}), bf16[256,2,768]{2,0,1:T(8,128)(2,1)}) %reduce-scatter.11.cloned.1.call-update) | async-done | bytes 786448 | tf_op jit(solution)/shard_map/reduce_scatter | solution.py:282
  553.0 2.1 fusion.70
  555.1 41.3 %all-reduce = (f32[4]{0:T(128)}, f32[768]{0:T(1024)}, f32[768]{0:T(1024)}, f32[768,16]{0,1:T(8,128)}, f32[4,16]{1,0:T(4,128)}) all-reduce(f32[4]{0:T(128)S(1)} %copy-done.113, f32[768]{0:T(1024)S(1)} %get-tuple-element.13, f32[768]{0:T(1024)S(1)} %copy-done.93, ...), channel_id=1, replica_groups=mesh['tensor'=4,'expert'=8] {'tensor','expert'}, use_global_device_ids=true, to_apply=%region_36.37 | all-reduce | flops 13892 | bytes 111136 | tf_op jit(solution)/shard_map/psum | solution.py:295
  596.4 3.3 fusion.59
  599.8 22.2 %all-reduce.4.cloned.1.call-done = (f32[3,768,192]{1,2,0:T(8,128)}, f32[192,768]{1,0:T(8,128)}) async-done(((f32[3,768,192]{1,2,0:T(8,128)}, f32[192,768]{1,0:T(8,128)}), (f32[3,768,192]{1,2,0:T(8,128)}, f32[192,768]{1,0:T(8,128)})) %all-reduce.4.cloned.1.call-update) | async-done | bytes 2359312 | tf_op jit(solution)/shard_map/psum | solution.py:280
  622.0 2.9 copy.92
  (378 shorter events, 64.2 us)
Async XLA Ops:
  7.2 196.5 %copy-start = (bf16[1,768,1536]{2,1,0:T(8,128)(2,1)S(1)}, bf16[1,768,1536]{2,1,0:T(8,128)(2,1)}, u32[]{:S(2)}) copy-start(bf16[1,768,1536]{2,1,0:T(8,128)(2,1)} %param.22) | copy-start | bytes 7077892
  7.2 54.0 %copy-start.124 = (bf16[3,768,192]{1,2,0:T(8,128)(2,1)S(1)}, bf16[3,768,192]{1,2,0:T(8,128)(2,1)}, u32[]{:S(2)}) copy-start(bf16[3,768,192]{1,2,0:T(8,128)(2,1)} %param.17) | copy-start | bytes 2654212
  7.2 54.0 %all-gather.3.cloned.1.call-start = ((), (), s32[]{:S(2)}) async-start(), calls=%async_computation.8 | async-start | bytes 3932160 | tf_op jit(solution)/shard_map/all_gather | solution.py:107
  14.4 142.4 %reduce-scatter.9.cloned.1.call-start = ((), (), s32[]{:S(2)}) async-start(), calls=%async_computation.9 | async-start | bytes 7864320 | tf_op jit(solution)/shard_map/reduce_scatter | solution.py:134
  65.1 14.9 %copy-start.10 = (bf16[2,1024,3,192]{1,3,2,0:T(8,128)(2,1)}, bf16[2,1024,3,192]{1,3,2,0:T(8,128)(2,1)S(1)}, u32[]{:S(2)}) copy-start(bf16[2,1024,3,192]{1,3,2,0:T(8,128)(2,1)S(1)} %fusion.49) | copy-start | bytes 7077892
  68.5 8.4 %copy-start.3 = (f32[3,512,1024]{2,1,0:T(8,128)}, f32[3,512,1024]{2,1,0:T(8,128)S(1)}, u32[]{:S(2)}) copy-start(f32[3,512,1024]{2,1,0:T(8,128)S(1)} %get-tuple-element.42) | copy-start | bytes 18874372
  68.5 8.4 %copy-start.46 = (f32[3,512]{1,0:T(4,128)}, f32[3,512]{1,0:T(4,128)S(1)}, u32[]{:S(2)}) copy-start(f32[3,512]{1,0:T(4,128)S(1)} %get-tuple-element.41) | copy-start | bytes 18436
  69.6 10.4 %copy-start.2 = (f32[3,512,1024]{2,1,0:T(8,128)}, f32[3,512,1024]{2,1,0:T(8,128)S(1)}, u32[]{:S(2)}) copy-start(f32[3,512,1024]{2,1,0:T(8,128)S(1)} %get-tuple-element.46) | copy-start | bytes 18874372
  69.6 10.4 %copy-start.48 = (f32[3,512]{1,0:T(4,128)}, f32[3,512]{1,0:T(4,128)S(1)}, u32[]{:S(2)}) copy-start(f32[3,512]{1,0:T(4,128)S(1)} %get-tuple-element.45) | copy-start | bytes 18436
  86.4 70.4 %copy-start.6 = (bf16[2,256,768]{2,1,0:T(8,128)(2,1)S(1)}, bf16[2,256,768]{2,1,0:T(8,128)(2,1)}, u32[]{:S(2)}) copy-start(bf16[2,256,768]{2,1,0:T(8,128)(2,1)} %param.12) | copy-start | bytes 2359300
  89.4 69.9 %copy-start.106 = (pred[512]{0:T(512)(128)(4,1)}, pred[512]{0:T(512)(128)(4,1)S(1)}, u32[]{:S(2)}) copy-start(pred[512]{0:T(512)(128)(4,1)S(1)} %broadcast_compare_fusion) | copy-start | bytes 1540
  89.4 182.1 %copy-start.105 = (s32[512]{0:T(512)}, s32[512]{0:T(512)S(1)}, u32[]{:S(2)}) copy-start(s32[512]{0:T(512)S(1)} %multiply_add_fusion.1) | copy-start | bytes 6148
  158.6 74.2 %copy-start.56 = (f32[1,2,2,128]{3,1,2,0:T(2,128)}, f32[1,2,2,128]{3,1,2,0:T(2,128)S(1)}, u32[]{:S(2)}) copy-start(f32[1,2,2,128]{3,1,2,0:T(2,128)S(1)} %copy.81) | copy-start | bytes 6148
  159.1 73.7 %copy-start.59 = (f32[512]{0:T(512)}, f32[512]{0:T(512)S(1)}, u32[]{:S(2)}) copy-start(f32[512]{0:T(512)S(1)} %rsqrt.45) | copy-start | bytes 6148
  203.7 18.1 %copy-start.21 = (bf16[8,128,768]{2,1,0:T(8,128)(2,1)}, bf16[8,128,768]{2,1,0:T(8,128)(2,1)S(1)}, u32[]{:S(2)}) copy-start(bf16[8,128,768]{2,1,0:T(8,128)(2,1)S(1)} %all_to_all.20) | copy-start | bytes 4718596
  203.7 19.8 %copy-start.122 = (bf16[1,768,1536]{2,1,0:T(8,128)(2,1)S(1)}, bf16[1,768,1536]{2,1,0:T(8,128)(2,1)}, u32[]{:S(2)}) copy-start(bf16[1,768,1536]{2,1,0:T(8,128)(2,1)} %param.23) | copy-start | bytes 7077892
  227.2 44.3 %copy-start.14 = (bf16[2,256,768]{2,1,0:T(8,128)(2,1)S(1)}, bf16[2,256,768]{2,1,0:T(8,128)(2,1)}, u32[]{:S(2)}) copy-start(bf16[2,256,768]{2,1,0:T(8,128)(2,1)} %param.13) | copy-start | bytes 2359300
  227.2 42.7 %all-to-all-start.1 = ((bf16[8,128,768]{2,1,0:T(8,128)(2,1)}), bf16[8,128,768]{2,1,0:T(8,128)(2,1)}, u32[]{:S(2)}, u32[]{:S(2)}) async-start(bf16[8,128,768]{2,1,0:T(8,128)(2,1)} %fusion.52), calls=%async_computation.2 | async-start | bytes 3145728 | tf_op jit(solution)/shard_map/all_to_all | solution.py:176
  232.1 41.9 %copy-start.80 = (f32[1,2,2,128]{3,1,2,0:T(2,128)}, f32[1,2,2,128]{3,1,2,0:T(2,128)S(1)}, u32[]{:S(2)}) copy-start(f32[1,2,2,128]{3,1,2,0:T(2,128)S(1)} %copy.84) | copy-start | bytes 6148
  235.9 138.6 %copy-start.35 = (f32[512,16]{0,1:T(8,128)}, f32[512,16]{0,1:T(8,128)S(1)}, u32[]{:S(2)}) copy-start(f32[512,16]{0,1:T(8,128)S(1)} %get-tuple-element.49) | copy-start | bytes 98308
  236.5 39.0 %copy-start.82 = (f32[512]{0:T(512)}, f32[512]{0:T(512)S(1)}, u32[]{:S(2)}) copy-start(f32[512]{0:T(512)S(1)} %add_rsqrt_fusion) | copy-start | bytes 6148
  236.7 38.8 %copy-start.73 = (f32[512,4]{0,1:T(4,128)}, f32[512,4]{0,1:T(4,128)S(1)}, u32[]{:S(2)}) copy-start(f32[512,4]{0,1:T(4,128)S(1)} %get-tuple-element.51) | copy-start | bytes 24580
  237.3 38.2 %copy-start.90 = (f32[512]{0:T(512)}, f32[512]{0:T(512)S(1)}, u32[]{:S(2)}) copy-start(f32[512]{0:T(512)S(1)} %fusion.197) | copy-start | bytes 6148
  275.6 40.5 %copy-start.123 = (bf16[1,768,1536]{2,1,0:T(8,128)(2,1)S(1)}, bf16[1,768,1536]{2,1,0:T(8,128)(2,1)}, u32[]{:S(2)}) copy-start(bf16[1,768,1536]{2,1,0:T(8,128)(2,1)} %param.23) | copy-start | bytes 7077892
  316.1 7.5 %copy-start.22 = (bf16[8,128,768]{2,1,0:T(8,128)(2,1)}, bf16[8,128,768]{2,1,0:T(8,128)(2,1)S(1)}, u32[]{:S(2)}) copy-start(bf16[8,128,768]{2,1,0:T(8,128)(2,1)S(1)} %all_to_all.21) | copy-start | bytes 4718596
  329.1 42.3 %all-to-all-start.3 = ((bf16[8,128,768]{2,1,0:T(8,128)(2,1)}), bf16[8,128,768]{2,1,0:T(8,128)(2,1)}, u32[]{:S(2)}, u32[]{:S(2)}) async-start(bf16[8,128,768]{2,1,0:T(8,128)(2,1)} %fusion.55), calls=%async_computation.4 | async-start | bytes 3145728 | tf_op jit(solution)/shard_map/all_to_all | solution.py:226
  333.5 41.0 %copy-start.9 = (f32[512,768]{1,0:T(8,128)S(1)}, f32[512,768]{1,0:T(8,128)}, u32[]{:S(2)}) copy-start(f32[512,768]{1,0:T(8,128)} %copy-done.8) | copy-start | bytes 4718596
  333.5 90.4 %all-gather.5.cloned.1.call-start = ((), (), s32[]{:S(2)}) async-start(), calls=%async_computation.10 | async-start | bytes 3932160 | tf_op jit(solution)/shard_map/all_gather | solution.py:244
  334.0 43.7 %copy-start.40 = (f32[512,16]{0,1:T(8,128)}, f32[512,16]{0,1:T(8,128)S(1)}, u32[]{:S(2)}) copy-start(f32[512,16]{0,1:T(8,128)S(1)} %get-tuple-element.55) | copy-start | bytes 98308
  381.9 96.8 %reduce-scatter.15.cloned.1.call-start = ((), (), s32[]{:S(2)}) async-start(), calls=%async_computation.13 | async-start | bytes 2949120
  393.0 111.5 %reduce-scatter.13.cloned.1.call-start = ((), (), s32[]{:S(2)}) async-start(), calls=%async_computation.12 | async-start | bytes 2949120
  404.0 147.4 %reduce-scatter.11.cloned.1.call-start = ((), (), s32[]{:S(2)}) async-start(), calls=%async_computation.11 | async-start | bytes 3932160 | tf_op jit(solution)/shard_map/reduce_scatter | solution.py:282
  427.1 23.2 %copy-start.15 = (bf16[2,1024,192]{1,2,0:T(8,128)(2,1)}, bf16[2,1024,192]{1,2,0:T(8,128)(2,1)S(1)}, u32[]{:S(2)}) copy-start(bf16[2,1024,192]{1,2,0:T(8,128)(2,1)S(1)} %convolution_convert_fusion.2) | copy-start | bytes 2359300
  427.1 9.6 %slice-start.2 = ((s8[6291456]{0:T(1024)(128)(4,1)}), s8[4194304]{0:T(1024)(128)(4,1)S(1)}, s32[]{:S(2)}) async-start(s8[6291456]{0:T(1024)(128)(4,1)} %bitcast.333), calls=%async_computation.17 | async-start | bytes 8388608
  441.6 8.7 %slice-start = ((s8[6291456]{0:T(1024)(128)(4,1)}), s8[4194304]{0:T(1024)(128)(4,1)S(1)}, s32[]{:S(2)}) async-start(s8[6291456]{0:T(1024)(128)(4,1)} %bitcast.331), calls=%async_computation.15 | async-start | bytes 8388608
  474.9 147.1 %all-reduce.4.cloned.1.call-start = ((), (), s32[]{:S(2)}) async-start(), calls=%async_computation.14 | async-start | bytes 4718592 | tf_op jit(solution)/shard_map/psum | solution.py:280
  478.7 29.4 %copy-start.18 = (bf16[1024,3,64]{0,2,1:T(8,128)(2,1)S(1)}, bf16[1024,3,64]{0,2,1:T(8,128)(2,1)}, u32[]{:S(2)}) copy-start(bf16[1024,3,64]{0,2,1:T(8,128)(2,1)} %copy-done.17) | copy-start | bytes 1179652
  478.7 29.4 %copy-start.20 = (bf16[1024,3,64]{0,2,1:T(8,128)(2,1)S(1)}, bf16[1024,3,64]{0,2,1:T(8,128)(2,1)}, u32[]{:S(2)}) copy-start(bf16[1024,3,64]{0,2,1:T(8,128)(2,1)} %copy-done.19) | copy-start | bytes 1179652
  510.4 41.0 %copy-start.7 = (bf16[2,256,768]{2,1,0:T(8,128)(2,1)S(1)}, bf16[2,256,768]{2,1,0:T(8,128)(2,1)}, u32[]{:S(2)}) copy-start(bf16[2,256,768]{2,1,0:T(8,128)(2,1)} %param.12) | copy-start | bytes 2359300
  510.4 41.0 %copy-start.53 = (f32[768]{0:T(1024)S(1)}, f32[768]{0:T(1024)}, u32[]{:S(2)}) copy-start(f32[768]{0:T(1024)} %param.16) | copy-start | bytes 9220
  510.4 41.0 %copy-start.55 = (f32[2,256]{1,0:T(2,128)S(1)}, f32[2,256]{1,0:T(2,128)}, u32[]{:S(2)}) copy-start(f32[2,256]{1,0:T(2,128)} %copy-done.54) | copy-start | bytes 6148
  513.8 39.2 %copy-start.87 = (f32[2,256]{1,0:T(2,128)S(1)}, f32[2,256]{1,0:T(2,128)}, u32[]{:S(2)}) copy-start(f32[2,256]{1,0:T(2,128)} %copy-done.86) | copy-start | bytes 6148
  513.8 39.2 %copy-start.79 = (f32[2,256]{1,0:T(2,128)S(1)}, f32[2,256]{1,0:T(2,128)}, u32[]{:S(2)}) copy-start(f32[2,256]{1,0:T(2,128)} %copy-done.78) | copy-start | bytes 6148
  513.8 41.3 %copy-start.39 = (f32[768,16]{0,1:T(8,128)S(1)}, f32[768,16]{0,1:T(8,128)}, u32[]{:S(2)}) copy-start(f32[768,16]{0,1:T(8,128)} %fusion.121) | copy-start | bytes 147460
  513.8 41.3 %copy-start.93 = (f32[768]{0:T(1024)S(1)}, f32[768]{0:T(1024)}, u32[]{:S(2)}) copy-start(f32[768]{0:T(1024)} %get-tuple-element.11) | copy-start | bytes 9220
  513.8 41.3 %copy-start.104 = (f32[4,16]{1,0:T(4,128)S(1)}, f32[4,16]{1,0:T(4,128)}, u32[]{:S(2)}) copy-start(f32[4,16]{1,0:T(4,128)} %add_add_fusion.6) | copy-start | bytes 772
  513.8 41.3 %copy-start.113 = (f32[4]{0:T(128)S(1)}, f32[4]{0:T(128)}, u32[]{:S(2)}) copy-start(f32[4]{0:T(128)} %convert_element_type.207) | copy-start | bytes 52
  596.4 29.2 %copy-start.1 = (bf16[1,768,1536]{2,1,0:T(8,128)(2,1)S(1)}, bf16[1,768,1536]{2,1,0:T(8,128)(2,1)}, u32[]{:S(2)}) copy-start(bf16[1,768,1536]{2,1,0:T(8,128)(2,1)} %param.22) | copy-start | bytes 7077892
  (97 other events, 284.2 us)
Sparse Core Ops, SparseCore 0:
  14.5 46.6 all-gather.2
  86.5 70.2 reduce-scatter.8
  382.0 41.8 all-gather.4
  426.8 37.3 reduce-scatter.14
  467.1 37.3 reduce-scatter.12
  507.4 43.9 reduce-scatter.10
  554.4 67.4 all-reduce.3
where the time goes:
time: 643 us; the launch traced here: 633 us
  waiting for transfers between devices  288 us (45%)
  blocking collectives  124 us (19%)
  matrix products  118 us (18%)
  other arithmetic  48.2 us (7%)
  local copies, waits for them, and re-layouts  29.3 us (5%)
  between operations  16.3 us (3%)
  starting transfers between devices  9.77 us (2%)
    reduce_scatter x1, waiting for transfers between devices, body(): lax.psum_scatter(jnp.einsum('slh,hd->lsd', piece, output_weight, preferre...  67.4 us
    all_gather x1, waiting for transfers between devices, body(): collected_rows = lax.all_gather(normed_low, 'tensor', axis=1, tiled=True)  46.8 us
    all_to_all x1, blocking collectives, body(): lax.all_to_all(pair_copy(sent.reshape(experts, capacity, features)), 'exp...  42.2 us
    psum x1, blocking collectives, body(): lax.psum((norm1_grad, norm2_grad, route_weight_grad, embed_grad, loads_lo...  41.3 us
    all_to_all x1, blocking collectives, body(): lax.all_to_all(pair_copy(grad_sent.reshape(experts, capacity, features)),...  40.4 us
    reduce_scatter x1, waiting for transfers between devices, body(): lax.psum_scatter(jnp.einsum('kslh,kdh->lsd', piece, query_key_value_weigh...  37.5 us
    all_to_all x1, waiting for transfers between devices, body(): lax.all_to_all(grad_slots.reshape(received.shape).astype(jnp.bfloat16), '...  36.7 us
    all_to_all x1, waiting for transfers between devices, body(): lax.all_to_all(returned.reshape(received.shape).astype(jnp.bfloat16), 'ex...  32.5 us
  transfers between devices with their start and end apart: 9, of which 8 were waited for; matrix products, arithmetic and copies ran while one was open for 15% of the time, Pallas kernels for 0%

commit v1 on v0

--- a/solution.py
+++ b/solution.py
@@ -3,6 +3,7 @@
 import jax.numpy as jnp
 from jax import lax
 from jax.sharding import PartitionSpec as P
+from jax.lax import psum
 
 HEAD = 64
 
@@ -292,8 +293,9 @@
     )
     input_grad = grad_hidden + grad_inputs_norm
     loads_local = jnp.sum(member, axis=0).astype(jnp.float32)
-    norm1_grad, norm2_grad, route_weight_grad, embed_grad, loads = lax.psum(
-        (norm1_grad, norm2_grad, route_weight_grad, embed_grad, loads_local), ("tensor", "expert")
+    norm1_grad, norm2_grad, route_weight_grad, embed_grad, loads = psum(
+        psum((norm1_grad, norm2_grad, route_weight_grad, embed_grad, loads_local), "expert"),
+        "tensor",
     )
     return (
         result.reshape(seq_count, shard_len, features),

time: 643 us -> 643 us (level)
    psum x1 -> x2, blocking collectives: 41.3 us -> 46.7 us  [the longest x1 29.9 us: body(): psum((norm1_grad, norm2_grad, route_weight_grad, embed_grad, loads_local)...]
where the time goes in v1:
time: 643 us; the launch traced here: 633 us
  waiting for transfers between devices  282 us (44%)
  blocking collectives  129 us (20%)
  matrix products  118 us (18%)
  other arithmetic  48.2 us (7%)
  local copies, waits for them, and re-layouts  29.4 us (5%)
  between operations  16.3 us (3%)
  starting transfers between devices  9.76 us (2%)
    reduce_scatter x1, waiting for transfers between devices, body(): lax.psum_scatter(jnp.einsum('slh,hd->lsd', piece, output_weight, preferre...  67.4 us
    all_gather x1, waiting for transfers between devices, body(): collected_rows = lax.all_gather(normed_low, 'tensor', axis=1, tiled=True)  46.8 us
    all_to_all x1, blocking collectives, body(): lax.all_to_all(pair_copy(sent.reshape(experts, capacity, features)), 'exp...  42.2 us
    all_to_all x1, blocking collectives, body(): lax.all_to_all(pair_copy(grad_sent.reshape(experts, capacity, features)),...  40.4 us
    reduce_scatter x1, waiting for transfers between devices, body(): lax.psum_scatter(jnp.einsum('kslh,kdh->lsd', piece, query_key_value_weigh...  37.5 us
    all_to_all x1, waiting for transfers between devices, body(): lax.all_to_all(grad_slots.reshape(received.shape).astype(jnp.bfloat16), '...  36.8 us
    all_to_all x1, waiting for transfers between devices, body(): lax.all_to_all(returned.reshape(received.shape).astype(jnp.bfloat16), 'ex...  32.5 us
    psum x1, blocking collectives, body(): psum((norm1_grad, norm2_grad, route_weight_grad, embed_grad, loads_local)...  29.9 us
  transfers between devices with their start and end apart: 9, of which 8 were waited for; matrix products, arithmetic and copies ran while one was open for 15% of the time, Pallas kernels for 0%

profile of v1, /device:TPU:0, one launch (start us, length us, event | category | flops | bytes accessed | tf_op | source)
XLA Modules:
  0.0 633.1 jit_solution(13159970204793569793)
XLA Ops:
  12.0 2.3 fusion.75
  14.4 46.8 %all-gather.3.cloned.1.call-done = bf16[2,1024,768]{2,1,0:T(8,128)(2,1)} async-done(((bf16[2,256,768]{2,1,0:T(8,128)(2,1)}), bf16[2,1024,768]{2,1,0:T(8,128)(2,1)}) %all-gather.3.cloned.1.call-update) | async-done | bytes 3145744 | tf_op jit(solution)/shard_map/all_gather | solution.py:108
  61.2 3.9 fusion.49
  76.9 1.8 fusion.107
  82.7 3.7 convolution_bitcast_fusion
  89.4 67.4 %reduce-scatter.9.cloned.1.call-done = f32[256,2,768]{2,0,1:T(8,128)} async-done(((f32[1024,2,768]{2,0,1:T(8,128)}), f32[256,2,768]{2,0,1:T(8,128)}) %reduce-scatter.9.cloned.1.call-update) | async-done | bytes 1572880 | tf_op jit(solution)/shard_map/reduce_scatter | solution.py:135
  156.8 1.8 fusion.113
  161.4 42.2 %all_to_all.20 = bf16[8,128,768]{2,1,0:T(8,128)(2,1)S(1)} all-to-all(bf16[8,128,768]{2,1,0:T(8,128)(2,1)S(1)} %bitcast.361), channel_id=1, replica_groups=mesh['tensor'=4,'expert'=8] {'expert'}, dimensions={0} | all-to-all | bytes 3145728 | tf_op jit(solution)/shard_map/all_to_all | solution.py:162
  203.7 18.1 %multiply_convert_fusion.4 = (bf16[1024,1536]{1,0:T(8,128)(2,1)S(1)}, f32[1024,1536]{1,0:T(8,128)}, f32[1024,1536]{1,0:T(8,128)}) fusion(bf16[1024,768]{1,0:T(8,128)(2,1)S(1)} %bitcast.378, bf16[1,768,1536]{2,1,0:T(8,128)(2,1)S(1)} %copy-done), kind=kOutput, calls=%fused_computation.16 | convolution fusion | flops 2518155264 | bytes 19660800 | tf_op jit(solution)/shard_map/dot_general | solution.py:171
  221.8 1.7 copy-done.126
  223.5 3.7 fusion.52
  227.2 4.9 all-to-all-start.1
  232.9 3.1 multiply_reduce_fusion.12
  237.4 32.5 %all-to-all-done.1 = bf16[8,128,768]{2,1,0:T(8,128)(2,1)} async-done(((bf16[8,128,768]{2,1,0:T(8,128)(2,1)}), bf16[8,128,768]{2,1,0:T(8,128)(2,1)}, u32[]{:S(2)}, u32[]{:S(2)}) %all-to-all-start.1) | async-done | bytes 1572896 | tf_op jit(solution)/shard_map/all_to_all | solution.py:177
  269.9 1.6 bitcast_reduce_fusion.1
  271.6 2.4 fusion.66
  275.7 40.4 %all_to_all.21 = bf16[8,128,768]{2,1,0:T(8,128)(2,1)S(1)} all-to-all(bf16[8,128,768]{2,1,0:T(8,128)(2,1)S(1)} %bitcast.362), channel_id=1, replica_groups=mesh['tensor'=4,'expert'=8] {'expert'}, dimensions={0} | all-to-all | bytes 3145728 | tf_op jit(solution)/shard_map/all_to_all | solution.py:200
  316.1 7.5 %add_convert_fusion = bf16[1024,1536]{1,0:T(8,128)(2,1)S(1)} fusion(f32[1024,1536]{1,0:T(8,128)} %get-tuple-element.34, f32[1024,1536]{1,0:T(8,128)} %get-tuple-element.52, bf16[1024,768]{1,0:T(8,128)(2,1)S(1)} %bitcast.380, bf16[1,768,1536]{2,1,0:T(8,128)(2,1)S(1)} %copy-done.123), kind=kOutput, calls=%fused_computation.15 | convolution fusion | flops 2437939200 | bytes 19660800 | tf_op jit(solution)/shard_map/dot_general | solution.py:208
  323.6 1.6 copy-done.127
  325.3 3.7 fusion.55
  329.1 4.4 all-to-all-start.3
  334.6 36.8 %all-to-all-done.3 = bf16[8,128,768]{2,1,0:T(8,128)(2,1)} async-done(((bf16[8,128,768]{2,1,0:T(8,128)(2,1)}), bf16[8,128,768]{2,1,0:T(8,128)(2,1)}, u32[]{:S(2)}, u32[]{:S(2)}) %all-to-all-start.3) | async-done | bytes 1572896 | tf_op jit(solution)/shard_map/all_to_all | solution.py:227
  374.5 3.1 multiply_reduce_fusion.8
  377.7 1.8 fusion.200
  382.1 6.4 %convolution_convert_fusion = bf16[768,1536]{1,0:T(8,128)(2,1)} fusion(bf16[1024,768]{1,0:T(8,128)(2,1)} %bitcast.381, bf16[1024,1536]{1,0:T(8,128)(2,1)} %copy-done.126), kind=kOutput, calls=%fused_computation.50 | convolution fusion | flops 2417098752 | bytes 7077888 | tf_op jit(solution)/shard_map/dot_general | solution.py:210
  388.6 4.5 copy.71
  393.2 6.4 %convolution_convert_fusion.1 = bf16[768,1536]{1,0:T(8,128)(2,1)} fusion(bf16[1024,768]{1,0:T(8,128)(2,1)} %bitcast.379, bf16[1024,1536]{1,0:T(8,128)(2,1)} %copy-done.127), kind=kOutput, calls=%fused_computation.51 | convolution fusion | flops 2417098752 | bytes 7077888 | tf_op jit(solution)/shard_map/dot_general | solution.py:213
  399.6 4.3 copy.69
  404.0 19.9 %all-gather.5.cloned.1.call-done = bf16[2,1024,768]{2,1,0:T(8,128)(2,1)} async-done(((bf16[2,256,768]{2,1,0:T(8,128)(2,1)}), bf16[2,1024,768]{2,1,0:T(8,128)(2,1)}) %all-gather.5.cloned.1.call-update) | async-done | bytes 3145744 | tf_op jit(solution)/shard_map/all_gather | solution.py:245
  423.9 3.2 convolution_convert_fusion.2
  427.2 4.3 multiply_reduce_fusion
  431.5 4.2 multiply_convert_fusion
  436.8 2.1 multiply_reduce_fusion.1
  441.6 3.8 multiply_reduce_fusion.2
  445.4 3.9 multiply_convert_fusion.2
  450.4 3.8 multiply_reduce_fusion.3
  454.9 3.8 multiply_convert_fusion.3
  470.5 4.1 fusion.22
  476.9 1.8 fusion.121
  480.2 24.4 %reduce-scatter.13.cloned.1.call-done = bf16[384,768]{1,0:T(8,128)(2,1)} async-done(((bf16[1536,768]{1,0:T(8,128)(2,1)}), bf16[384,768]{1,0:T(8,128)(2,1)}) %reduce-scatter.13.cloned.1.call-update) | async-done | bytes 589840
  510.4 3.4 fusion.78
  513.9 37.5 %reduce-scatter.11.cloned.1.call-done = bf16[256,2,768]{2,0,1:T(8,128)(2,1)} async-done(((bf16[1024,2,768]{2,0,1:T(8,128)(2,1)}), bf16[256,2,768]{2,0,1:T(8,128)(2,1)}) %reduce-scatter.11.cloned.1.call-update) | async-done | bytes 786448 | tf_op jit(solution)/shard_map/reduce_scatter | solution.py:283
  553.1 2.1 fusion.70
  555.2 29.9 %all-reduce = (f32[4]{0:T(128)S(1)}, f32[768]{0:T(1024)S(1)}, f32[768]{0:T(1024)S(1)}, f32[768,16]{0,1:T(8,128)S(1)}, f32[4,16]{1,0:T(4,128)S(1)}) all-reduce(f32[4]{0:T(128)S(1)} %copy-done.113, f32[768]{0:T(1024)S(1)} %get-tuple-element.13, f32[768]{0:T(1024)S(1)} %copy-done.93, ...), channel_id=1, replica_groups=mesh['tensor'=4,'expert'=8] {'expert'}, use_global_device_ids=true, to_apply=%region_36.37 | all-reduce | flops 13892 | bytes 111136 | tf_op jit(solution)/shard_map/psum | solution.py:297
  585.1 16.8 %all-reduce.2 = (f32[4]{0:T(128)}, f32[768]{0:T(1024)}, f32[768]{0:T(1024)}, f32[768,16]{0,1:T(8,128)}, f32[4,16]{1,0:T(4,128)}) all-reduce(f32[4]{0:T(128)S(1)} %get-tuple-element.19, f32[768]{0:T(1024)S(1)} %get-tuple-element.20, f32[768]{0:T(1024)S(1)} %get-tuple-element.21, ...), channel_id=1, replica_groups=mesh['tensor'=4,'expert'=8] {'tensor'}, use_global_device_ids=true, to_apply=%region_37.38 | all-reduce | flops 13892 | bytes 111136 | tf_op jit(solution)/shard_map/psum | solution.py:296
  601.9 3.4 fusion.59
  605.2 16.9 %all-reduce.5.cloned.1.call-done = (f32[3,768,192]{1,2,0:T(8,128)}, f32[192,768]{1,0:T(8,128)}) async-done(((f32[3,768,192]{1,2,0:T(8,128)}, f32[192,768]{1,0:T(8,128)}), (f32[3,768,192]{1,2,0:T(8,128)}, f32[192,768]{1,0:T(8,128)})) %all-reduce.5.cloned.1.call-update) | async-done | bytes 2359312 | tf_op jit(solution)/shard_map/psum | solution.py:281
  622.1 2.9 copy.92
  (379 shorter events, 65.8 us)
Async XLA Ops:
  7.2 196.5 %copy-start = (bf16[1,768,1536]{2,1,0:T(8,128)(2,1)S(1)}, bf16[1,768,1536]{2,1,0:T(8,128)(2,1)}, u32[]{:S(2)}) copy-start(bf16[1,768,1536]{2,1,0:T(8,128)(2,1)} %param.22) | copy-start | bytes 7077892
  7.2 54.0 %copy-start.124 = (bf16[3,768,192]{1,2,0:T(8,128)(2,1)S(1)}, bf16[3,768,192]{1,2,0:T(8,128)(2,1)}, u32[]{:S(2)}) copy-start(bf16[3,768,192]{1,2,0:T(8,128)(2,1)} %param.17) | copy-start | bytes 2654212
  7.2 54.0 %all-gather.3.cloned.1.call-start = ((), (), s32[]{:S(2)}) async-start(), calls=%async_computation.8 | async-start | bytes 3932160 | tf_op jit(solution)/shard_map/all_gather | solution.py:108
  14.4 142.4 %reduce-scatter.9.cloned.1.call-start = ((), (), s32[]{:S(2)}) async-start(), calls=%async_computation.9 | async-start | bytes 7864320 | tf_op jit(solution)/shard_map/reduce_scatter | solution.py:135
  65.1 14.9 %copy-start.10 = (bf16[2,1024,3,192]{1,3,2,0:T(8,128)(2,1)}, bf16[2,1024,3,192]{1,3,2,0:T(8,128)(2,1)S(1)}, u32[]{:S(2)}) copy-start(bf16[2,1024,3,192]{1,3,2,0:T(8,128)(2,1)S(1)} %fusion.49) | copy-start | bytes 7077892
  68.5 8.4 %copy-start.3 = (f32[3,512,1024]{2,1,0:T(8,128)}, f32[3,512,1024]{2,1,0:T(8,128)S(1)}, u32[]{:S(2)}) copy-start(f32[3,512,1024]{2,1,0:T(8,128)S(1)} %get-tuple-element.47) | copy-start | bytes 18874372
  68.5 8.4 %copy-start.46 = (f32[3,512]{1,0:T(4,128)}, f32[3,512]{1,0:T(4,128)S(1)}, u32[]{:S(2)}) copy-start(f32[3,512]{1,0:T(4,128)S(1)} %get-tuple-element.46) | copy-start | bytes 18436
  69.6 10.4 %copy-start.2 = (f32[3,512,1024]{2,1,0:T(8,128)}, f32[3,512,1024]{2,1,0:T(8,128)S(1)}, u32[]{:S(2)}) copy-start(f32[3,512,1024]{2,1,0:T(8,128)S(1)} %get-tuple-element.51) | copy-start | bytes 18874372
  69.6 10.4 %copy-start.48 = (f32[3,512]{1,0:T(4,128)}, f32[3,512]{1,0:T(4,128)S(1)}, u32[]{:S(2)}) copy-start(f32[3,512]{1,0:T(4,128)S(1)} %get-tuple-element.50) | copy-start | bytes 18436
  86.4 70.4 %copy-start.6 = (bf16[2,256,768]{2,1,0:T(8,128)(2,1)S(1)}, bf16[2,256,768]{2,1,0:T(8,128)(2,1)}, u32[]{:S(2)}) copy-start(bf16[2,256,768]{2,1,0:T(8,128)(2,1)} %param.12) | copy-start | bytes 2359300
  89.4 69.9 %copy-start.106 = (pred[512]{0:T(512)(128)(4,1)}, pred[512]{0:T(512)(128)(4,1)S(1)}, u32[]{:S(2)}) copy-start(pred[512]{0:T(512)(128)(4,1)S(1)} %broadcast_compare_fusion) | copy-start | bytes 1540
  89.4 182.1 %copy-start.105 = (s32[512]{0:T(512)}, s32[512]{0:T(512)S(1)}, u32[]{:S(2)}) copy-start(s32[512]{0:T(512)S(1)} %multiply_add_fusion.1) | copy-start | bytes 6148
  158.6 74.3 %copy-start.56 = (f32[1,2,2,128]{3,1,2,0:T(2,128)}, f32[1,2,2,128]{3,1,2,0:T(2,128)S(1)}, u32[]{:S(2)}) copy-start(f32[1,2,2,128]{3,1,2,0:T(2,128)S(1)} %copy.81) | copy-start | bytes 6148
  159.1 73.7 %copy-start.59 = (f32[512]{0:T(512)}, f32[512]{0:T(512)S(1)}, u32[]{:S(2)}) copy-start(f32[512]{0:T(512)S(1)} %rsqrt.45) | copy-start | bytes 6148
  203.7 18.1 %copy-start.21 = (bf16[8,128,768]{2,1,0:T(8,128)(2,1)}, bf16[8,128,768]{2,1,0:T(8,128)(2,1)S(1)}, u32[]{:S(2)}) copy-start(bf16[8,128,768]{2,1,0:T(8,128)(2,1)S(1)} %all_to_all.20) | copy-start | bytes 4718596
  203.7 19.8 %copy-start.122 = (bf16[1,768,1536]{2,1,0:T(8,128)(2,1)S(1)}, bf16[1,768,1536]{2,1,0:T(8,128)(2,1)}, u32[]{:S(2)}) copy-start(bf16[1,768,1536]{2,1,0:T(8,128)(2,1)} %param.23) | copy-start | bytes 7077892
  227.2 44.3 %copy-start.14 = (bf16[2,256,768]{2,1,0:T(8,128)(2,1)S(1)}, bf16[2,256,768]{2,1,0:T(8,128)(2,1)}, u32[]{:S(2)}) copy-start(bf16[2,256,768]{2,1,0:T(8,128)(2,1)} %param.13) | copy-start | bytes 2359300
  227.2 42.7 %all-to-all-start.1 = ((bf16[8,128,768]{2,1,0:T(8,128)(2,1)}), bf16[8,128,768]{2,1,0:T(8,128)(2,1)}, u32[]{:S(2)}, u32[]{:S(2)}) async-start(bf16[8,128,768]{2,1,0:T(8,128)(2,1)} %fusion.52), calls=%async_computation.2 | async-start | bytes 3145728 | tf_op jit(solution)/shard_map/all_to_all | solution.py:177
  232.1 41.9 %copy-start.80 = (f32[1,2,2,128]{3,1,2,0:T(2,128)}, f32[1,2,2,128]{3,1,2,0:T(2,128)S(1)}, u32[]{:S(2)}) copy-start(f32[1,2,2,128]{3,1,2,0:T(2,128)S(1)} %copy.84) | copy-start | bytes 6148
  236.0 138.5 %copy-start.35 = (f32[512,16]{0,1:T(8,128)}, f32[512,16]{0,1:T(8,128)S(1)}, u32[]{:S(2)}) copy-start(f32[512,16]{0,1:T(8,128)S(1)} %get-tuple-element.54) | copy-start | bytes 98308
  236.6 39.0 %copy-start.82 = (f32[512]{0:T(512)}, f32[512]{0:T(512)S(1)}, u32[]{:S(2)}) copy-start(f32[512]{0:T(512)S(1)} %add_rsqrt_fusion) | copy-start | bytes 6148
  236.8 38.7 %copy-start.73 = (f32[512,4]{0,1:T(4,128)}, f32[512,4]{0,1:T(4,128)S(1)}, u32[]{:S(2)}) copy-start(f32[512,4]{0,1:T(4,128)S(1)} %get-tuple-element.56) | copy-start | bytes 24580
  237.4 38.1 %copy-start.90 = (f32[512]{0:T(512)}, f32[512]{0:T(512)S(1)}, u32[]{:S(2)}) copy-start(f32[512]{0:T(512)S(1)} %fusion.197) | copy-start | bytes 6148
  275.6 40.5 %copy-start.123 = (bf16[1,768,1536]{2,1,0:T(8,128)(2,1)S(1)}, bf16[1,768,1536]{2,1,0:T(8,128)(2,1)}, u32[]{:S(2)}) copy-start(bf16[1,768,1536]{2,1,0:T(8,128)(2,1)} %param.23) | copy-start | bytes 7077892
  316.1 7.5 %copy-start.22 = (bf16[8,128,768]{2,1,0:T(8,128)(2,1)}, bf16[8,128,768]{2,1,0:T(8,128)(2,1)S(1)}, u32[]{:S(2)}) copy-start(bf16[8,128,768]{2,1,0:T(8,128)(2,1)S(1)} %all_to_all.21) | copy-start | bytes 4718596
  329.1 42.3 %all-to-all-start.3 = ((bf16[8,128,768]{2,1,0:T(8,128)(2,1)}), bf16[8,128,768]{2,1,0:T(8,128)(2,1)}, u32[]{:S(2)}, u32[]{:S(2)}) async-start(bf16[8,128,768]{2,1,0:T(8,128)(2,1)} %fusion.55), calls=%async_computation.4 | async-start | bytes 3145728 | tf_op jit(solution)/shard_map/all_to_all | solution.py:227
  333.5 41.0 %copy-start.9 = (f32[512,768]{1,0:T(8,128)S(1)}, f32[512,768]{1,0:T(8,128)}, u32[]{:S(2)}) copy-start(f32[512,768]{1,0:T(8,128)} %copy-done.8) | copy-start | bytes 4718596
  333.5 90.4 %all-gather.5.cloned.1.call-start = ((), (), s32[]{:S(2)}) async-start(), calls=%async_computation.10 | async-start | bytes 3932160 | tf_op jit(solution)/shard_map/all_gather | solution.py:245
  334.0 43.7 %copy-start.40 = (f32[512,16]{0,1:T(8,128)}, f32[512,16]{0,1:T(8,128)S(1)}, u32[]{:S(2)}) copy-start(f32[512,16]{0,1:T(8,128)S(1)} %get-tuple-element.60) | copy-start | bytes 98308
  381.9 96.9 %reduce-scatter.15.cloned.1.call-start = ((), (), s32[]{:S(2)}) async-start(), calls=%async_computation.13 | async-start | bytes 2949120
  393.0 111.6 %reduce-scatter.13.cloned.1.call-start = ((), (), s32[]{:S(2)}) async-start(), calls=%async_computation.12 | async-start | bytes 2949120
  404.0 147.4 %reduce-scatter.11.cloned.1.call-start = ((), (), s32[]{:S(2)}) async-start(), calls=%async_computation.11 | async-start | bytes 3932160 | tf_op jit(solution)/shard_map/reduce_scatter | solution.py:283
  427.1 23.2 %copy-start.15 = (bf16[2,1024,192]{1,2,0:T(8,128)(2,1)}, bf16[2,1024,192]{1,2,0:T(8,128)(2,1)S(1)}, u32[]{:S(2)}) copy-start(bf16[2,1024,192]{1,2,0:T(8,128)(2,1)S(1)} %convolution_convert_fusion.2) | copy-start | bytes 2359300
  427.2 9.6 %slice-start.2 = ((s8[6291456]{0:T(1024)(128)(4,1)}), s8[4194304]{0:T(1024)(128)(4,1)S(1)}, s32[]{:S(2)}) async-start(s8[6291456]{0:T(1024)(128)(4,1)} %bitcast.333), calls=%async_computation.17 | async-start | bytes 8388608
  441.6 8.7 %slice-start = ((s8[6291456]{0:T(1024)(128)(4,1)}), s8[4194304]{0:T(1024)(128)(4,1)S(1)}, s32[]{:S(2)}) async-start(s8[6291456]{0:T(1024)(128)(4,1)} %bitcast.331), calls=%async_computation.15 | async-start | bytes 8388608
  474.9 147.3 %all-reduce.5.cloned.1.call-start = ((), (), s32[]{:S(2)}) async-start(), calls=%async_computation.14 | async-start | bytes 4718592 | tf_op jit(solution)/shard_map/psum | solution.py:281
  478.7 29.5 %copy-start.18 = (bf16[1024,3,64]{0,2,1:T(8,128)(2,1)S(1)}, bf16[1024,3,64]{0,2,1:T(8,128)(2,1)}, u32[]{:S(2)}) copy-start(bf16[1024,3,64]{0,2,1:T(8,128)(2,1)} %copy-done.17) | copy-start | bytes 1179652
  478.7 29.5 %copy-start.20 = (bf16[1024,3,64]{0,2,1:T(8,128)(2,1)S(1)}, bf16[1024,3,64]{0,2,1:T(8,128)(2,1)}, u32[]{:S(2)}) copy-start(bf16[1024,3,64]{0,2,1:T(8,128)(2,1)} %copy-done.19) | copy-start | bytes 1179652
  510.4 41.0 %copy-start.7 = (bf16[2,256,768]{2,1,0:T(8,128)(2,1)S(1)}, bf16[2,256,768]{2,1,0:T(8,128)(2,1)}, u32[]{:S(2)}) copy-start(bf16[2,256,768]{2,1,0:T(8,128)(2,1)} %param.12) | copy-start | bytes 2359300
  510.4 41.0 %copy-start.53 = (f32[768]{0:T(1024)S(1)}, f32[768]{0:T(1024)}, u32[]{:S(2)}) copy-start(f32[768]{0:T(1024)} %param.16) | copy-start | bytes 9220
  510.4 41.0 %copy-start.55 = (f32[2,256]{1,0:T(2,128)S(1)}, f32[2,256]{1,0:T(2,128)}, u32[]{:S(2)}) copy-start(f32[2,256]{1,0:T(2,128)} %copy-done.54) | copy-start | bytes 6148
  513.8 39.2 %copy-start.87 = (f32[2,256]{1,0:T(2,128)S(1)}, f32[2,256]{1,0:T(2,128)}, u32[]{:S(2)}) copy-start(f32[2,256]{1,0:T(2,128)} %copy-done.86) | copy-start | bytes 6148
  513.8 39.2 %copy-start.79 = (f32[2,256]{1,0:T(2,128)S(1)}, f32[2,256]{1,0:T(2,128)}, u32[]{:S(2)}) copy-start(f32[2,256]{1,0:T(2,128)} %copy-done.78) | copy-start | bytes 6148
  513.8 41.3 %copy-start.39 = (f32[768,16]{0,1:T(8,128)S(1)}, f32[768,16]{0,1:T(8,128)}, u32[]{:S(2)}) copy-start(f32[768,16]{0,1:T(8,128)} %fusion.121) | copy-start | bytes 147460
  513.8 41.3 %copy-start.93 = (f32[768]{0:T(1024)S(1)}, f32[768]{0:T(1024)}, u32[]{:S(2)}) copy-start(f32[768]{0:T(1024)} %get-tuple-element.11) | copy-start | bytes 9220
  513.8 41.3 %copy-start.104 = (f32[4,16]{1,0:T(4,128)S(1)}, f32[4,16]{1,0:T(4,128)}, u32[]{:S(2)}) copy-start(f32[4,16]{1,0:T(4,128)} %add_add_fusion.6) | copy-start | bytes 772
  513.9 41.3 %copy-start.113 = (f32[4]{0:T(128)S(1)}, f32[4]{0:T(128)}, u32[]{:S(2)}) copy-start(f32[4]{0:T(128)} %convert_element_type.207) | copy-start | bytes 52
  601.9 23.9 %copy-start.1 = (bf16[1,768,1536]{2,1,0:T(8,128)(2,1)S(1)}, bf16[1,768,1536]{2,1,0:T(8,128)(2,1)}, u32[]{:S(2)}) copy-start(bf16[1,768,1536]{2,1,0:T(8,128)(2,1)} %param.22) | copy-start | bytes 7077892
  (97 other events, 284.2 us)
Sparse Core Ops, SparseCore 0:
  14.5 46.6 all-gather.2
  86.5 70.2 reduce-scatter.8
  382.0 41.8 all-gather.4
  426.8 37.3 reduce-scatter.14
  467.2 37.3 reduce-scatter.12
  507.4 43.9 reduce-scatter.10
  554.5 67.6 all-reduce.4
